TPU v7x, 128 devices: a whole 4x4x4 slice. The times are simulated.
128 devices in a mesh: grp: 16 (over y, x), lag: 8 (over z, core).
Axes of the slice: x: 4, y: 4, z: 4, core: 2. Of those that a mesh axis runs over, the one named last changes fastest.
Arguments:
- weights: bfloat16 [3, 16384, 256], P(None, 'lag'), may hold values from -0.125 to 0.125
- history: bfloat16 [512, 2048, 256], P(('grp', 'lag')), may hold values from -6 to 6
- send_patch: int32 [2048, 2], P(('grp', 'lag')), may hold values from 0 to 3
- send_lag: int32 [2048, 2], P(('grp', 'lag')), may hold values from 0 to 56
- send_class: int32 [2048, 2], P(('grp', 'lag')), may hold values from 0 to 2
- recv_target: int32 [2048, 2], P(('grp', 'lag')), may hold values from 0 to 3
- local_src: int32 [6144], P(('grp', 'lag')), may hold values from 0 to 3
- local_lag: int32 [6144], P(('grp', 'lag')), may hold values from 0 to 56
- local_class: int32 [6144], P(('grp', 'lag')), may hold values from 0 to 2
- local_target: int32 [6144], P(('grp', 'lag')), may hold values from 0 to 3
- inverse_blocks: bfloat16 [512, 256, 256], P(('grp', 'lag')), may hold values from -0.375 to 0.375
- incident: bfloat16 [512, 256, 256], P(('grp', 'lag')), may hold values from -6 to 6
Outputs:
- density: bfloat16 [512, 256, 256], P(('grp', 'lag'))
All inputs are finite; a program needn't handle non-finite values.
Results may differ from a plain program's by a relative error of at most 0.0049.
Values may be sent and summed in bfloat16 or wider, within the bound.
A program may use at most 256 MiB of HBM per device.

v0:
```python
import jax
import jax.numpy as jnp
from jax import lax
from jax.sharding import PartitionSpec as P


def pair_product(gathered, source, key, klass, offset):
    panel_count = gathered.shape[2]
    height = source.shape[1]
    window = lax.dynamic_slice(
        gathered, (klass, offset * panel_count, jnp.int32(0)), (1, height, panel_count)
    )[0]
    rows = lax.dynamic_index_in_dim(source, key, 0, keepdims=False)
    return lax.dot_general(
        window, rows, (((0,), (0,)), ((), ())), preferred_element_type=jnp.float32
    )


def block_width():
    return 8


def block_products(gathered, source, block_keys, block_classes, block_offsets):
    outputs = [
        pair_product(gathered, source, block_keys[i], block_classes[i], block_offsets[i])
        for i in range(block_keys.shape[0])
    ]
    return jnp.stack(outputs, 0)


def compute_pairs(gathered, source, keys, classes, offsets):
    total = keys.shape[0]
    width = block_width()

    def compute_step(carry, inputs):
        block_keys, block_classes, block_offsets = inputs
        return (carry, block_products(gathered, source, block_keys, block_classes, block_offsets))

    _, result = lax.scan(
        compute_step,
        jnp.int32(0),
        (keys.reshape(-1, width), classes.reshape(-1, width), offsets.reshape(-1, width)),
    )
    return result.reshape(total, result.shape[2], result.shape[3])


def collect(owned, targets, contrib):
    select = (jnp.arange(owned, dtype=jnp.int32)[:, None] == targets[None, :]).astype(jnp.float32)
    return jnp.einsum("ts,spc->tpc", select, contrib, precision=lax.Precision.HIGHEST)


def accumulate_pairs(gathered, source, keys, classes, offsets, targets, initial):
    width = block_width()
    owned = initial.shape[0]

    def accumulate_step(carry, inputs):
        block_keys, block_classes, block_offsets, block_targets = inputs
        contrib = block_products(gathered, source, block_keys, block_classes, block_offsets)
        return (carry + collect(owned, block_targets, contrib), None)

    result, _ = lax.scan(
        accumulate_step,
        initial,
        (
            keys.reshape(-1, width),
            classes.reshape(-1, width),
            offsets.reshape(-1, width),
            targets.reshape(-1, width),
        ),
    )
    return result


def per_device(
    weights,
    history,
    send_patch,
    send_lag,
    send_class,
    recv_target,
    local_src,
    local_lag,
    local_class,
    local_target,
    inverse_blocks,
    incident,
):
    owned = history.shape[0]
    panel_count = weights.shape[2]
    excite = history.shape[2]
    peers = send_patch.shape[0]
    slots = send_patch.shape[1]
    gathered = lax.all_gather(weights, "lag", axis=1, tiled=True)
    computed = compute_pairs(
        gathered,
        history,
        send_patch.reshape(peers * slots),
        send_class.reshape(peers * slots),
        send_lag.reshape(peers * slots),
    )
    remote = lax.all_to_all(
        computed.reshape(peers, slots, panel_count, excite),
        "grp",
        split_axis=0,
        concat_axis=0,
        tiled=True,
    )
    near_start = jnp.zeros((owned, panel_count, excite), jnp.float32)
    near_sum = accumulate_pairs(
        gathered, history, local_src, local_class, local_lag, local_target, near_start
    )
    near_sum = near_sum + collect(
        owned,
        recv_target.reshape(peers * slots),
        remote.reshape(peers * slots, panel_count, excite),
    )
    residual = (incident.astype(jnp.float32) - near_sum).astype(jnp.bfloat16)
    density = jnp.einsum(
        "tpq,tqc->tpc", inverse_blocks, residual, preferred_element_type=jnp.float32
    )
    return density.astype(jnp.bfloat16)


def solution(mesh):
    return jax.shard_map(
        per_device,
        mesh=mesh,
        in_specs=(
            P(None, "lag", None),
            P(("grp", "lag"), None, None),
            P(("grp", "lag"), None),
            P(("grp", "lag"), None),
            P(("grp", "lag"), None),
            P(("grp", "lag"), None),
            P(("grp", "lag")),
            P(("grp", "lag")),
            P(("grp", "lag")),
            P(("grp", "lag")),
            P(("grp", "lag"), None, None),
            P(("grp", "lag"), None, None),
        ),
        out_specs=P(("grp", "lag"), None, None),
        check_vma=False,
    )
```

profile of v0, /device:TPU:1, one launch (start us, length us, event | category | flops | bytes accessed | tf_op | source)
XLA Modules:
  0.0 721.8 jit_solution(8559357001827942845)
XLA Ops:
  13.6 119.5 %all-gather.2.cloned.1.call-done = bf16[3,16384,256]{2,1,0:T(8,128)(2,1)} async-done(((bf16[3,2048,256]{2,1,0:T(8,128)(2,1)}), bf16[3,16384,256]{2,1,0:T(8,128)(2,1)}) %all-gather.2.cloned.1.call-update) | async-done | bytes 25165840 | tf_op jit(solution)/shard_map/all_gather | solution.py:93
  133.1 216.0 %while.21 = (s32[]{:T(128)}, f32[4,8,256,256]{3,2,1,0:T(8,128)}, s32[4,8]{1,0:T(4,128)S(1)}, s32[4,8]{1,0:T(4,128)S(1)}, bf16[3,16384,256]{2,1,0:T(8,128)(2,1)},...) while((s32[]{:T(128)}, f32[4,8,256,256]{3,2,1,0:T(8,128)}, ...), condition=%wide.region_3.4_spmd, body=%wide.region_2.3_spmd.sunk | while | flops 2147483648 | bytes 23070708 | solution.py:39
  171.0 2.0 fusion.210
  183.6 2.0 fusion.212
  199.7 2.0 fusion.206
  225.0 2.0 fusion.210
  237.6 2.0 fusion.212
  279.0 2.0 fusion.210
  291.6 2.0 fusion.212
  307.8 2.0 fusion.206
  326.6 2.0 fusion.209
  333.0 2.0 fusion.210
  345.6 2.0 fusion.212
  349.1 6.6 all-to-all-start
  355.7 346.6 %while.22 = (s32[]{:T(128)}, f32[4,256,256]{2,0,1:T(4,128)}, s32[6,8]{1,0:T(8,128)S(1)}, s32[6,8]{1,0:T(8,128)S(1)}, s32[6,8]{1,0:T(8,128)S(1)}, /*index=5*/bf16...) while((s32[]{:T(128)}, f32[4,256,256]{2,0,1:T(4,128)}, ...), condition=%wide.region_1.2_spmd.clone, body=%wide.region_0.1_spmd.clone.sunk | while | flops 2173173760 | bytes 23070312 | solution.py:61
  375.3 2.0 fusion.236
  381.8 2.0 fusion.237
  388.1 2.0 fusion.238
  400.6 2.0 fusion.240
  407.1 2.0 fusion.241
  409.1 3.4 fusion.243
  432.0 2.0 fusion.236
  444.9 2.0 fusion.238
  457.3 2.0 fusion.240
  463.8 2.0 fusion.241
  465.9 4.6 fusion.243
  490.0 2.0 fusion.236
  496.6 2.0 fusion.237
  502.8 2.0 fusion.238
  515.3 2.0 fusion.240
  521.8 2.0 fusion.241
  523.9 4.6 fusion.243
  547.9 2.0 fusion.236
  560.8 2.0 fusion.238
  573.2 2.0 fusion.240
  579.8 2.0 fusion.241
  581.8 4.6 fusion.243
  605.9 2.0 fusion.236
  618.8 2.0 fusion.238
  631.2 2.0 fusion.240
  637.7 2.0 fusion.241
  639.8 4.6 fusion.243
  663.9 2.0 fusion.236
  676.7 2.0 fusion.238
  689.1 2.0 fusion.240
  695.7 2.0 fusion.241
  697.7 4.6 fusion.243
  702.3 11.2 %fusion.113 = bf16[4,256,256]{2,0,1:T(4,128)(2,1)S(1)} fusion(f32[4,256,256]{2,0,1:T(4,128)} %get-tuple-element.84, f32[32,256,256]{2,1,0:T(8,128)} %bitcast.51, bf16[4,256,256]{2,1,0:T(8,128)(2,1)S(1)} %copy-done.1, s32[32]{0:T(128)S(1)} %eq.31), kind=kOutput, calls=%fused_computation.131 | convolution fusion | flops 101712000 | bytes 10485888 | tf_op jit(solution)/shard_map/ts,spc->tpc/dot_general | solution.py:49
  (126 shorter events, 121.8 us)
Async XLA Ops:
  6.5 707.0 %copy-start = (bf16[4,256,256]{2,1,0:T(8,128)(2,1)S(1)}, bf16[4,256,256]{2,1,0:T(8,128)(2,1)}, u32[]{:S(2)}) copy-start(bf16[4,256,256]{2,1,0:T(8,128)(2,1)} %param.26) | copy-start | bytes 1572868
  6.5 126.6 %all-gather.2.cloned.1.call-start = ((), (), s32[]{:S(2)}) async-start(), calls=%async_computation.1 | async-start | bytes 28311552 | tf_op jit(solution)/shard_map/all_gather | solution.py:93
  349.1 353.2 %all-to-all-start = ((f32[16,2,256,256]{3,2,1,0:T(8,128)}), f32[16,2,256,256]{3,2,1,0:T(8,128)}, u32[]{:S(2)}, u32[]{:S(2)}) async-start(f32[16,2,256,256]{3,2,1,0:T(8,128)} %bitcast.421), calls=%async_computation | async-start | bytes 16777216 | tf_op jit(solution)/shard_map/all_to_all | solution.py:101
  355.7 346.6 %copy-start.1 = (bf16[4,256,256]{2,1,0:T(8,128)(2,1)S(1)}, bf16[4,256,256]{2,1,0:T(8,128)(2,1)}, u32[]{:S(2)}) copy-start(bf16[4,256,256]{2,1,0:T(8,128)(2,1)} %param.27) | copy-start | bytes 1572868
Sparse Core Ops, SparseCore 0:
  9.1 124.0 all-gather.1
where the time goes:
time: 730 us; the launch traced here: 722 us
  loops' own time  348 us (48%)
  matrix products  200 us (27%)
  waiting for transfers between devices  120 us (16%)
  local copies, waits for them, and re-layouts  33.7 us (5%)
  between operations  13.4 us (2%)
    another operation x1, loops' own time, accumulate_pairs(): lax.scan(accumulate_step, initial, (keys.reshape(-1, width), classes.resh...  211 us
    dot_general x80, matrix products, pair_product(): lax.dot_general(window, rows, (((0,), (0,)), ((), ())), preferred_element...  162 us
    another operation x1, loops' own time, compute_pairs(): lax.scan(compute_step, jnp.int32(0), (keys.reshape(-1, width), classes.re...  137 us
    all_gather x1, waiting for transfers between devices, per_device(): gathered = lax.all_gather(weights, 'lag', axis=1, tiled=True)  120 us
    dot_general x7, matrix products, collect(): jnp.einsum('ts,spc->tpc', select, contrib, precision=lax.Precision.HIGHEST)  37.5 us
  transfers between devices with their start and end apart: 2, of which 1 were waited for; matrix products, arithmetic and copies ran while one was open for 20% of the time, Pallas kernels for 0%

commit v1 on v0

v1 whole, which is shorter than its diff:
```python
import jax
import jax.numpy as jnp
from jax import lax
from jax.experimental import pallas as pl
from jax.experimental.pallas import tpu as pltpu
from jax.sharding import PartitionSpec as P

MESH = pl.DeviceIdType.MESH
PANEL = 256
STEPS = 8
LAGS = 64
OWN_LAGS = 8
CLASSES = 3
OWNED = 4
SIDE = 4
SLOTS = 2
NLOC = 48
GROUP = 8


def near_kernel(
    w_hbm, h_hbm, send_patch, send_lag, send_class, recv_target,
    local_src, local_lag, local_class, local_target,
    near_ref,
    table, hist_t, hist_in, send_buf, recv_buf, merged, arrived, contrib, target_own, target_row,
    send_sem, recv_sem, pair_send, pair_recv, load_sem, hist_sem,
):
    grp = lax.axis_index("grp")
    lag = lax.axis_index("lag")
    core = lax.rem(lag, 2)
    zpos = lag // 2
    xpos = lax.rem(grp, SIDE)
    ypos = grp // SIDE
    a_pos = jnp.where(core == 0, xpos, ypos)
    b_pos = jnp.where(core == 0, ypos, xpos)
    a_unit = jnp.where(core == 0, 1, SIDE)
    b_unit = jnp.where(core == 0, SIDE, 1)

    def at(pos, step):
        return lax.rem(pos + step, SIDE)

    def device(da=0, db=0, dz=0):
        return (at(a_pos, da) * a_unit + at(b_pos, db) * b_unit, at(zpos, dz) * 2 + core)

    twin = (grp, zpos * 2 + 1 - core)

    sizes = []

    def send(src, dst, to):
        n = len(sizes)
        sizes.append(src)
        pltpu.make_async_remote_copy(
            src_ref=src, dst_ref=dst, send_sem=send_sem.at[n], recv_sem=recv_sem.at[n],
            device_id=to, device_id_type=MESH,
        ).start()
        return n

    def arrive(n, ref):
        pltpu.make_async_remote_copy(
            src_ref=ref, dst_ref=ref, send_sem=send_sem.at[n], recv_sem=recv_sem.at[n],
            device_id=twin, device_id_type=MESH,
        ).wait_recv()

    def sent(n, ref):
        pltpu.make_async_remote_copy(
            src_ref=ref, dst_ref=ref, send_sem=send_sem.at[n], recv_sem=recv_sem.at[n],
            device_id=twin, device_id_type=MESH,
        ).wait_send()

    def shard(dz, c=None):
        return at(zpos, dz) * 2 + (core if c is None else c)

    def direct(dz, half=None, c=None):
        start = shard(dz, c) * OWN_LAGS
        if half is None:
            return table.at[pl.ds(start, 8)]
        return table.at[pl.ds(start + 4 * half, 4)]

    def one(dz, da):
        s = b_pos * SIDE + at(a_pos, da)
        return table.at[pl.ds((1 + s // 8) * LAGS + shard(dz) * OWN_LAGS + lax.rem(s, 8), 1)]

    def row(dz, db, half=None, bb=None, c=None):
        b = at(b_pos, db) if bb is None else bb
        start = (1 + b // 2) * LAGS + shard(dz, c) * OWN_LAGS + lax.rem(b, 2) * 4
        if half is None:
            return table.at[pl.ds(start, 4)]
        return table.at[pl.ds(start + 2 * half, 2)]

    loads = [
        pltpu.make_async_copy(
            w_hbm.at[pl.ds(k * OWN_LAGS, OWN_LAGS)],
            table.at[pl.ds(k * LAGS + lag * OWN_LAGS, OWN_LAGS)],
            load_sem.at[k],
        )
        for k in range(CLASSES)
    ]
    hist = [
        pltpu.make_async_copy(h_hbm.at[s], hist_in.at[s % 2], hist_sem.at[s]) for s in range(OWNED)
    ]
    hist[0].start()
    hist[1].start()

    barrier = pltpu.get_barrier_semaphore()
    partners = [twin]
    for d in (1, 2, 3):
        partners += [device(da=d), device(db=d), device(dz=d)]
    for p in partners:
        pl.semaphore_signal(barrier, inc=1, device_id=p, device_id_type=MESH)

    for b in range(SIDE):
        for a in range(SIDE):
            for s in range(SLOTS):
                value = recv_target[a * a_unit + b * b_unit, s]
                target_own[b, pl.ds(a * SLOTS + s, 1), :] = jnp.full((1, PANEL), value, jnp.int32)
    target_row[3] = target_own[b_pos]
    pl.semaphore_wait(barrier, len(partners))

    own = b_pos * SIDE + a_pos
    slice_id = {}
    for dz in (1, 3, 2):
        slice_id[dz] = send(w_hbm.at[pl.ds(8 + own, 1)], one(0, 0), device(dz=dz))
    direct_id = {}
    for first in (True, False):
        for dz in (1, 3):
            half = (0 if dz == 1 else 1) if first else (1 if dz == 1 else 0)
            direct_id[dz, half] = send(w_hbm.at[pl.ds(4 * half, 4)], direct(0, half), device(dz=dz))
    target_id = {}
    for dd in (1, 2, 3):
        target_id[3 - dd] = send(target_own.at[at(b_pos, dd)], target_row.at[3 - dd], device(db=dd))
    for copy in loads:
        copy.start()
    twin_in = []
    for k in range(CLASSES):
        n = send(
            w_hbm.at[pl.ds(k * OWN_LAGS, OWN_LAGS)],
            table.at[pl.ds(k * LAGS + lag * OWN_LAGS, OWN_LAGS)],
            twin,
        )
        twin_in.append((n, table.at[pl.ds(k * LAGS + shard(0, 1 - core) * OWN_LAGS, OWN_LAGS)]))

    def turn(s):
        hist[s].wait()

        @pl.loop(0, STEPS)
        def _(m):
            block = hist_in[s % 2, pl.ds(pl.multiple_of(m * PANEL, PANEL), PANEL), :]
            hist_t[s, :, pl.ds(pl.multiple_of(m * PANEL, PANEL), PANEL)] = block.T

    turn(0)
    hist[2].start()
    turn(1)
    hist[3].start()

    first_id = {}
    for dz in (1, 3, 2):
        arrive(slice_id[dz], one(-dz % 4, 0))
        for da in (1, 3, 2):
            first_id[dz, da] = send(one(-dz % 4, 0), one(-dz % 4, 0), device(da=da))
    turn(2)
    turn(3)
    zero = jnp.zeros((PANEL, PANEL), jnp.float32)
    for t in range(OWNED):
        near_ref[t] = zero

    second_id = {}
    for dz in (1, 3, 2):
        for da in (1, 3, 2):
            arrive(first_id[dz, da], one(-dz % 4, -da % 4))
        for db, half in ((1, 0), (3, 1), (1, 1), (3, 0)):
            second_id[dz, db, half] = send(row(-dz % 4, 0, half), row(-dz % 4, 0, half), device(db=db))
        n = send(row(-dz % 4, 0), row(-dz % 4, 0), twin)
        twin_in.append((n, row(-dz % 4, 0, bb=jnp.where(core == 0, xpos, ypos), c=1 - core)))

    relay_id = {}
    for dz, half in ((1, 0), (3, 1)):
        arrive(direct_id[dz, half], direct(-dz % 4, half))
        relay_id[dz] = send(direct(-dz % 4, half), direct(-dz % 4, half), device(dz=dz))
    for dz, half in ((1, 1), (3, 0)):
        arrive(direct_id[dz, half], direct(-dz % 4, half))
        n = send(direct(-dz % 4), direct(-dz % 4), twin)
        twin_in.append((n, direct(-dz % 4, c=1 - core)))

    pass_id = {}
    for dz in (1, 3, 2):
        for db, half in ((1, 0), (3, 1)):
            arrive(second_id[dz, db, half], row(-dz % 4, -db % 4, half))
            pass_id[dz, db] = send(row(-dz % 4, -db % 4, half), row(-dz % 4, -db % 4, half), device(db=db))
        for db, half in ((1, 1), (3, 0)):
            arrive(second_id[dz, db, half], row(-dz % 4, -db % 4, half))
            n = send(row(-dz % 4, -db % 4), row(-dz % 4, -db % 4), twin)
            other = at(a_pos, -db % 4)
            twin_in.append((n, row(-dz % 4, 0, bb=other, c=1 - core)))
    for dz, half in ((1, 0), (3, 1)):
        arrive(relay_id[dz], direct(2, half))
    n = send(direct(2), direct(2), twin)
    twin_in.append((n, direct(2, c=1 - core)))
    for dz in (1, 3, 2):
        for db, half in ((1, 0), (3, 1)):
            arrive(pass_id[dz, db], row(-dz % 4, 2, half))
        n = send(row(-dz % 4, 2), row(-dz % 4, 2), twin)
        twin_in.append((n, row(-dz % 4, 0, bb=at(a_pos, 2), c=1 - core)))
    for n, ref in twin_in:
        arrive(n, ref)
    for copy in loads:
        copy.wait()

    def product(klass, offset, patch):
        window = table[pl.ds(klass * LAGS + offset, STEPS)].reshape(STEPS * PANEL, PANEL)
        return jnp.dot(hist_t[patch], window, preferred_element_type=jnp.float32)

    def pair_copy(q):
        da = lax.rem(lax.rem(q, 4) + 1, 4)
        return pltpu.make_async_remote_copy(
            src_ref=send_buf.at[pl.ds(q * SLOTS, SLOTS)], dst_ref=recv_buf.at[pl.ds(q * SLOTS, SLOTS)],
            send_sem=pair_send.at[q], recv_sem=pair_recv.at[q],
            device_id=device(da=da), device_id_type=MESH,
        )

    @pl.loop(0, SIDE * SIDE)
    def _(q):
        db = q // 4
        da = lax.rem(lax.rem(q, 4) + 1, 4)
        peer = at(a_pos, da) * a_unit + at(b_pos, db + 1) * b_unit
        for s in range(SLOTS):
            block = product(send_class[peer, s], send_lag[peer, s], send_patch[peer, s])
            send_buf[q * SLOTS + s] = block.astype(jnp.bfloat16)

        @pl.when(da != 0)
        def _():
            pair_copy(q).start()

    def local(first, count):
        @pl.loop(first, first + count)
        def _(group):
            @pl.loop(0, GROUP)
            def _(i):
                j = group * GROUP + i
                contrib[i] = product(local_class[j], local_lag[j], local_src[j])

            @pl.loop(0, PANEL // 8)
            def _(chunk):
                rows = pl.ds(pl.multiple_of(chunk * 8, 8), 8)
                parts = [contrib[i, rows, :] for i in range(GROUP)]
                for t in range(OWNED):
                    total = near_ref[t, rows, :]
                    for i in range(GROUP):
                        total += jnp.where(local_target[group * GROUP + i] == t, parts[i], 0.0)
                    near_ref[t, rows, :] = total

    def merge(db):
        for r in range(3):
            pair_copy(db * 4 + r).wait_recv()

        @pl.loop(0, PANEL // 16)
        def _(chunk):
            rows = pl.ds(pl.multiple_of(chunk * 16, 16), 16)
            totals = [None] * OWNED
            for r in range(4):
                da = (r + 1) % 4
                source = at(a_pos, -da % 4)
                buffer = send_buf if da == 0 else recv_buf
                for s in range(SLOTS):
                    part = buffer[(db * 4 + r) * SLOTS + s, rows, :].astype(jnp.float32)
                    which = target_row[db, pl.ds(source * SLOTS + s, 1), :]
                    for t in range(OWNED):
                        kept = jnp.where(jnp.broadcast_to(which, part.shape) == t, part, 0.0)
                        totals[t] = kept if totals[t] is None else totals[t] + kept
            for t in range(OWNED):
                if db < 3:
                    merged[db * OWNED + t, rows, :] = totals[t].astype(jnp.bfloat16)
                else:
                    near_ref[t, rows, :] += totals[t]

    def merged_copy(db):
        return pltpu.make_async_remote_copy(
            src_ref=merged.at[pl.ds(db * OWNED, OWNED)], dst_ref=arrived.at[pl.ds(db * OWNED, OWNED)],
            send_sem=pair_send.at[16 + db], recv_sem=pair_recv.at[16 + db],
            device_id=device(db=db + 1), device_id_type=MESH,
        )

    for db in range(3):
        arrive(target_id[db], target_row.at[db])
    for db in range(3):
        merge(db)
        merged_copy(db).start()
        local(2 * db, 2)
    merge(3)
    for db in range(3):
        merged_copy(db).wait_recv()

    @pl.loop(0, PANEL // 16)
    def _(chunk):
        rows = pl.ds(pl.multiple_of(chunk * 16, 16), 16)
        for t in range(OWNED):
            total = near_ref[t, rows, :]
            for db in range(3):
                total += arrived[db * OWNED + t, rows, :].astype(jnp.float32)
            near_ref[t, rows, :] = total

    for db in range(4):
        for r in range(3):
            pair_copy(db * 4 + r).wait_send()
    for db in range(3):
        merged_copy(db).wait_send()
    for n, ref in enumerate(sizes):
        sent(n, ref)


def near_field(weights, history, tables):
    vmem = pltpu.VMEM
    smem = pl.BlockSpec(memory_space=pltpu.SMEM)
    anywhere = pl.BlockSpec(memory_space=pl.ANY)
    return pl.pallas_call(
        near_kernel,
        out_shape=jax.ShapeDtypeStruct((OWNED, PANEL, PANEL), jnp.float32),
        in_specs=[anywhere, anywhere] + [smem] * 8,
        out_specs=pl.BlockSpec(memory_space=vmem),
        scratch_shapes=[
            vmem((CLASSES * LAGS, PANEL, PANEL), jnp.bfloat16),
            vmem((OWNED, PANEL, STEPS * PANEL), jnp.bfloat16),
            vmem((2, STEPS * PANEL, PANEL), jnp.bfloat16),
            vmem((32, PANEL, PANEL), jnp.bfloat16),
            vmem((32, PANEL, PANEL), jnp.bfloat16),
            vmem((12, PANEL, PANEL), jnp.bfloat16),
            vmem((12, PANEL, PANEL), jnp.bfloat16),
            vmem((GROUP, PANEL, PANEL), jnp.float32),
            vmem((SIDE, SIDE * SLOTS, PANEL), jnp.int32),
            vmem((SIDE, SIDE * SLOTS, PANEL), jnp.int32),
            pltpu.SemaphoreType.DMA((80,)),
            pltpu.SemaphoreType.DMA((80,)),
            pltpu.SemaphoreType.DMA((19,)),
            pltpu.SemaphoreType.DMA((19,)),
            pltpu.SemaphoreType.DMA((CLASSES,)),
            pltpu.SemaphoreType.DMA((OWNED,)),
        ],
        compiler_params=pltpu.CompilerParams(
            collective_id=0, has_side_effects=True, vmem_limit_bytes=60 * 2**20
        ),
    )(weights.reshape(CLASSES * OWN_LAGS, PANEL, PANEL), history, *tables)


def per_device(
    weights, history, send_patch, send_lag, send_class, recv_target,
    local_src, local_lag, local_class, local_target, inverse_blocks, incident,
):
    near_t = near_field(
        weights, history,
        (send_patch, send_lag, send_class, recv_target, local_src, local_lag, local_class, local_target),
    )
    near_sum = jnp.swapaxes(near_t, 1, 2)
    residual = (incident.astype(jnp.float32) - near_sum).astype(jnp.bfloat16)
    density = jnp.einsum("tpq,tqc->tpc", inverse_blocks, residual, preferred_element_type=jnp.float32)
    return density.astype(jnp.bfloat16)


def solution(mesh):
    both = ("grp", "lag")
    return jax.shard_map(
        per_device,
        mesh=mesh,
        in_specs=(
            P(None, "lag", None), P(both, None, None),
            P(both, None), P(both, None), P(both, None), P(both, None),
            P(both), P(both), P(both), P(both),
            P(both, None, None), P(both, None, None),
        ),
        out_specs=P(both, None, None),
        check_vma=False,
    )
```

time: 730 us -> 116 us (0.16); the launches traced: 722 us -> 115 us
  loops' own time: 348 us -> 0 us
  matrix products: 200 us -> 1.57 us
  waiting for transfers between devices: 120 us -> 0 us
  Pallas kernels: 0 us -> 106 us
  local copies, waits for them, and re-layouts: 33.7 us -> 7.7 us
  between operations: 13.4 us -> 0.03 us
    another operation x2 -> x0, loops' own time: 348 us -> none  [the longest x1 211 us: accumulate_pairs(): lax.scan(accumulate_step, initial, (keys.reshape(-1, width), classes.resh...]
    dot_general x87 -> x0, matrix products: 200 us -> none  [the longest x80 162 us: pair_product(): lax.dot_general(window, rows, (((0,), (0,)), ((), ())), preferred_element...]
    all_gather x1 -> x0, waiting for transfers between devices: 120 us -> none  [per_device(): gathered = lax.all_gather(weights, 'lag', axis=1, tiled=True)]
    pallas_call x0 -> x1, Pallas kernels: none -> 106 us  [near_field(): pl.pallas_call(near_kernel, out_shape=jax.ShapeDtypeStruct((OWNED, PANEL,...]
    slice x30 -> x0, local copies, waits for them, and re-layouts: 20.2 us -> none  [the longest x10 6.77 us: block_products(): block_keys[i]]
  transfers between devices with their start and end apart: 2 -> 0, of which waited for: 1 -> 0; matrix products, arithmetic and copies ran while one was open for 20% -> 0% of each run, Pallas kernels for 0% -> 0%
where the time goes in v1:
time: 116 us; the launch traced here: 115 us
  Pallas kernels  106 us (91%)
  local copies, waits for them, and re-layouts  7.7 us (7%)
  matrix products  1.57 us (1%)
    pallas_call x1, Pallas kernels, near_field(): pl.pallas_call(near_kernel, out_shape=jax.ShapeDtypeStruct((OWNED, PANEL,...  106 us
    unnamed x7, local copies, waits for them, and re-layouts  6.7 us

profile of v1, /device:TPU:1, one launch (start us, length us, event | category | flops | bytes accessed | tf_op | source)
XLA Modules:
  0.0 115.3 jit_solution(3378131489291155311)
XLA Ops:
  0.0 0.0 copy-start
  0.0 1.4 %copy.14.send_patch = s32[16,2]{1,0:T(8,128)} copy(s32[16,2]{0,1:T(2,128)} %param.14) | data formatting | bytes 256 | tf_op args[2]
  1.4 1.4 %copy.15.send_lag = s32[16,2]{1,0:T(8,128)} copy(s32[16,2]{0,1:T(2,128)} %param.15) | data formatting | bytes 256 | tf_op args[3]
  2.8 1.3 %copy.16.send_class = s32[16,2]{1,0:T(8,128)} copy(s32[16,2]{0,1:T(2,128)} %param.16) | data formatting | bytes 256 | tf_op args[4]
  4.1 1.4 %copy.17.recv_target = s32[16,2]{1,0:T(8,128)} copy(s32[16,2]{0,1:T(2,128)} %param.17) | data formatting | bytes 256 | tf_op args[5]
  5.5 1.2 %copy.13 = bf16[4,256,256]{1,2,0:T(8,128)(2,1)S(1)} copy(bf16[4,256,256]{2,1,0:T(8,128)(2,1)} %param.23) | data formatting | bytes 1048576 | tf_op args[11]
  6.7 106.0 %shard_map.118 = f32[4,256,256]{2,1,0:T(8,128)} custom-call(bf16[24,256,256]{2,1,0:T(8,128)(2,1)} %bitcast.9, bf16[4,2048,256]{2,1,0:T(8,128)(2,1)} %h_hbm.1, s32[16,2]{1,0:T(8,128)} %copy.14.send_patch, s32[16,2]{1,0:T(8,128)} %copy.15.send_lag, s32[16,2]{1,0:T(8,128)} %copy.16.send_class, s32[16,2]{1,0:T(8,128)} %copy.17.recv_target, s32[48]{0:T(128)} %local_src.1, ...), custom_call_target="tpu_custom_call" | custom-call | tf_op jit(solution)/shard_map/pallas_call | solution.py:314
  112.7 0.0 copy-done
  112.7 1.6 %fusion = bf16[4,256,256]{1,2,0:T(8,128)(2,1)S(1)} fusion(bf16[4,256,256]{2,1,0:T(8,128)(2,1)S(1)} %copy-done, f32[4,256,256]{2,1,0:T(8,128)} %shard_map.118, bf16[4,256,256]{1,2,0:T(8,128)(2,1)S(1)} %copy.13), kind=kOutput, calls=%fused_computation.1 | convolution fusion | flops 135266304 | bytes 2621440 | tf_op jit(solution)/shard_map/tpq,tqc->tpc/dot_general | solution.py:353
  114.3 1.0 copy.18
Async XLA Ops:
  0.0 112.7 %copy-start = (bf16[4,256,256]{2,1,0:T(8,128)(2,1)S(1)}, bf16[4,256,256]{2,1,0:T(8,128)(2,1)}, u32[]{:S(2)}) copy-start(bf16[4,256,256]{2,1,0:T(8,128)(2,1)} %param.22) | copy-start | bytes 1572868

commit v2 on v1

--- a/solution.py
+++ b/solution.py
@@ -111,7 +111,7 @@
     for b in range(SIDE):
         for a in range(SIDE):
             for s in range(SLOTS):
-                value = recv_target[a * a_unit + b * b_unit, s]
+                value = recv_target[s, a * a_unit + b * b_unit]
                 target_own[b, pl.ds(a * SLOTS + s, 1), :] = jnp.full((1, PANEL), value, jnp.int32)
     target_row[3] = target_own[b_pos]
     pl.semaphore_wait(barrier, len(partners))
@@ -223,7 +223,7 @@
         da = lax.rem(lax.rem(q, 4) + 1, 4)
         peer = at(a_pos, da) * a_unit + at(b_pos, db + 1) * b_unit
         for s in range(SLOTS):
-            block = product(send_class[peer, s], send_lag[peer, s], send_patch[peer, s])
+            block = product(send_class[s, peer], send_lag[s, peer], send_patch[s, peer])
             send_buf[q * SLOTS + s] = block.astype(jnp.bfloat16)
 
         @pl.when(da != 0)
@@ -238,15 +238,17 @@
                 j = group * GROUP + i
                 contrib[i] = product(local_class[j], local_lag[j], local_src[j])
 
-            @pl.loop(0, PANEL // 8)
+            @pl.loop(0, PANEL // 32)
             def _(chunk):
-                rows = pl.ds(pl.multiple_of(chunk * 8, 8), 8)
-                parts = [contrib[i, rows, :] for i in range(GROUP)]
+                rows = pl.ds(pl.multiple_of(chunk * 32, 32), 32)
+                totals = [near_ref[t, rows, :] for t in range(OWNED)]
+                for i in range(GROUP):
+                    part = contrib[i, rows, :]
+                    target = local_target[group * GROUP + i]
+                    for t in range(OWNED):
+                        totals[t] += jnp.where(target == t, part, 0.0)
                 for t in range(OWNED):
-                    total = near_ref[t, rows, :]
-                    for i in range(GROUP):
-                        total += jnp.where(local_target[group * GROUP + i] == t, parts[i], 0.0)
-                    near_ref[t, rows, :] = total
+                    near_ref[t, rows, :] = totals[t]
 
     def merge(db):
         for r in range(3):
@@ -346,7 +348,7 @@
 ):
     near_t = near_field(
         weights, history,
-        (send_patch, send_lag, send_class, recv_target, local_src, local_lag, local_class, local_target),
+        (send_patch.T, send_lag.T, send_class.T, recv_target.T, local_src, local_lag, local_class, local_target),
     )
     near_sum = jnp.swapaxes(near_t, 1, 2)
     residual = (incident.astype(jnp.float32) - near_sum).astype(jnp.bfloat16)

time: 116 us -> 104 us (0.90)
  Pallas kernels: 106 us -> 100 us
  local copies, waits for them, and re-layouts: 7.7 us -> 2.31 us
    pallas_call x1, Pallas kernels: 106 us -> 100 us  [near_field(): pl.pallas_call(near_kernel, out_shape=jax.ShapeDtypeStruct((OWNED, PANEL,...]
    unnamed x7 -> x3, local copies, waits for them, and re-layouts: 6.7 us -> 1.31 us
where the time goes in v2:
time: 104 us
  Pallas kernels  100 us (96%)
  local copies, waits for them, and re-layouts  2.31 us (2%)
  matrix products  1.56 us (2%)
    pallas_call x1, Pallas kernels, near_field(): pl.pallas_call(near_kernel, out_shape=jax.ShapeDtypeStruct((OWNED, PANEL,...  100 us

profile of v2, /device:TPU:1, one launch (start us, length us, event | category | flops | bytes accessed | tf_op | source)
XLA Modules:
  0.0 104.1 jit_solution(17944405045761156484)
XLA Ops:
  0.0 0.0 copy-start
  0.0 1.3 %copy.13 = bf16[4,256,256]{1,2,0:T(8,128)(2,1)S(1)} copy(bf16[4,256,256]{2,1,0:T(8,128)(2,1)} %param.23) | data formatting | bytes 1048576 | tf_op args[11]
  1.3 100.2 %shard_map.118 = f32[4,256,256]{2,1,0:T(8,128)} custom-call(bf16[24,256,256]{2,1,0:T(8,128)(2,1)} %bitcast.13, bf16[4,2048,256]{2,1,0:T(8,128)(2,1)} %h_hbm.1, s32[2,16]{1,0:T(2,128)} %bitcast.14, s32[2,16]{1,0:T(2,128)} %bitcast.15, s32[2,16]{1,0:T(2,128)} %bitcast.16, s32[2,16]{1,0:T(2,128)} %bitcast.17, s32[48]{0:T(128)} %local_src.1, s32[48]{0:T(128)} %local_lag.1, ...), custom_call_target="tpu_custom_call" | custom-call | tf_op jit(solution)/shard_map/pallas_call | solution.py:316
  101.5 0.0 copy-done
  101.6 1.6 %fusion = bf16[4,256,256]{1,2,0:T(8,128)(2,1)S(1)} fusion(bf16[4,256,256]{2,1,0:T(8,128)(2,1)S(1)} %copy-done, f32[4,256,256]{2,1,0:T(8,128)} %shard_map.118, bf16[4,256,256]{1,2,0:T(8,128)(2,1)S(1)} %copy.13), kind=kOutput, calls=%fused_computation.1 | convolution fusion | flops 135266304 | bytes 2621440 | tf_op jit(solution)/shard_map/tpq,tqc->tpc/dot_general | solution.py:355
  103.1 1.0 copy.14
Async XLA Ops:
  0.0 101.5 %copy-start = (bf16[4,256,256]{2,1,0:T(8,128)(2,1)S(1)}, bf16[4,256,256]{2,1,0:T(8,128)(2,1)}, u32[]{:S(2)}) copy-start(bf16[4,256,256]{2,1,0:T(8,128)(2,1)} %param.22) | copy-start | bytes 1572868

commit v3 on v2

v3 whole, which is shorter than its diff:
```python
import jax
import jax.numpy as jnp
from jax import lax
from jax.experimental import pallas as pl
from jax.experimental.pallas import tpu as pltpu
from jax.sharding import PartitionSpec as P

MESH = pl.DeviceIdType.MESH
PANEL = 256
STEPS = 8
LAGS = 64
OWN_LAGS = 8
CLASSES = 3
OWNED = 4
SIDE = 4
SLOTS = 2
NLOC = 48
GROUP = 8
HALF = 128
SHARD = 2048
PIECE_ROWS = (32, 16)
CHUNKS = (4, 2)
NCOPY = 112


def near_kernel(
    w_hbm, h_hbm, inverse_hbm, incident_hbm, send_patch, send_lag, send_class, recv_target,
    local_src, local_lag, local_class, local_target,
    out_ref,
    table0, table1, hist, shard_in, inverse, incident, near, send_buf, recv_buf, merged, arrived, contrib,
    target_own, target_row,
    send_sem, recv_sem, pair_send, pair_recv, load_sem,
):
    tables = (table0, table1)
    grp = lax.axis_index("grp")
    lag = lax.axis_index("lag")
    core = lax.rem(lag, 2)
    zpos = lag // 2
    xpos = lax.rem(grp, SIDE)
    ypos = grp // SIDE
    a_pos = jnp.where(core == 0, xpos, ypos)
    b_pos = jnp.where(core == 0, ypos, xpos)
    a_unit = jnp.where(core == 0, 1, SIDE)
    b_unit = jnp.where(core == 0, SIDE, 1)

    def at(pos, step):
        return lax.rem(pos + step % SIDE, SIDE)

    def device(da=0, db=0, dz=0):
        return (at(a_pos, da) * a_unit + at(b_pos, db) * b_unit, at(zpos, dz) * 2 + core)

    twin = (grp, zpos * 2 + 1 - core)

    copies = []

    def remote(n, src, dst, to):
        return pltpu.make_async_remote_copy(
            src_ref=src, dst_ref=dst, send_sem=send_sem.at[n], recv_sem=recv_sem.at[n],
            device_id=to, device_id_type=MESH,
        )

    def send(ref, to):
        n = len(copies)
        copies.append(ref)
        remote(n, ref, ref, to).start()
        return n

    def arrive(n, ref):
        remote(n, ref, ref, twin).wait_recv()

    def shard(dz, c=None):
        return at(zpos, dz) * 2 + (core if c is None else c)

    def piece(x, l, b, chunk=None):
        rows = PIECE_ROWS[x]
        count = OWN_LAGS if chunk is None else OWN_LAGS // CHUNKS[x]
        start = l * OWN_LAGS + (0 if chunk is None else chunk * count)
        return tables[x].at[:, pl.ds(start, count), pl.ds(pl.multiple_of(b * rows, rows), rows)]

    def deep(l, half=None):
        count = OWN_LAGS if half is None else OWN_LAGS // 2
        start = l * OWN_LAGS + (0 if half is None else half * count)
        return table1.at[:, pl.ds(start, count), pl.ds(HALF // 2, HALF // 2)]

    def whole(x, l):
        return tables[x].at[:, pl.ds(l * OWN_LAGS, OWN_LAGS)]

    shard_loads = [
        pltpu.make_async_copy(
            w_hbm.at[:, pl.ds(c * 512, 512)], shard_in.at[:, pl.ds(c * 512, 512)], load_sem.at[4 + c]
        )
        for c in range(4)
    ]
    hist_load = pltpu.make_async_copy(h_hbm, hist, load_sem.at[1])
    inverse_load = pltpu.make_async_copy(inverse_hbm, inverse, load_sem.at[2])
    incident_load = pltpu.make_async_copy(incident_hbm, incident, load_sem.at[3])
    for c in (0, 3, 1, 2):
        shard_loads[c].start()

    barrier = pltpu.get_barrier_semaphore()
    partners = [twin]
    for d in (1, 2, 3):
        partners += [device(da=d), device(db=d), device(dz=d)]
    for p in partners:
        pl.semaphore_signal(barrier, inc=1, device_id=p, device_id_type=MESH)

    for b in range(SIDE):
        for a in range(SIDE):
            for s in range(SLOTS):
                value = recv_target[s, a * a_unit + b * b_unit]
                target_own[b, pl.ds(a * SLOTS + s, 1), :] = jnp.full((1, PANEL), value, jnp.int32)
    target_row[3] = target_own[b_pos]

    def turn(x, c):
        @pl.loop(0, 2 * CLASSES)
        def _(n):
            i = 2 * c + lax.rem(n, 2)
            rows = pl.ds(pl.multiple_of(i * PANEL, PANEL), PANEL)
            tables[x][n // 2, lag * OWN_LAGS + i] = shard_in[n // 2, rows, pl.ds(x * HALF, HALF)].T

    z_id, relay_id, b_id, pass_id, deep_id, target_id = {}, {}, {}, {}, {}, {}
    twin_in = ([], [])

    def to_twin(x, ref, there):
        twin_in[x].append((send(ref, twin), there))

    def passed_on(x, step, chunk):
        return chunk < CHUNKS[x] // 2 if step == 1 else chunk >= CHUNKS[x] // 2

    def order(x, step):
        n = CHUNKS[x]
        if step == 1:
            return list(range(n))
        if step == 3:
            return list(range(n))[::-1]
        return [c for i in range(n // 2) for c in (i, n - 1 - i)]

    def z_send(x):
        for pair in zip(order(x, 1), order(x, 3)):
            for dz, c in zip((1, 3), pair):
                z_id[x, dz, c] = send(piece(x, lag, b_pos, c), device(dz=dz))

    def b_send(x, dz, c):
        for db in (1, 3):
            b_id[x, dz, db, c] = send(piece(x, shard(dz), b_pos, c), device(db=db))

    def z_recv(x):
        for pair in zip(order(x, 1), order(x, 3)):
            for dz, c in zip((1, 3), pair):
                ref = piece(x, shard(-dz), b_pos, c)
                arrive(z_id[x, dz, c], ref)
                if passed_on(x, dz, c):
                    relay_id[x, c] = send(ref, device(dz=dz))
                b_send(x, -dz % 4, c)

    def z_relay_recv(x):
        for c in order(x, 2):
            arrive(relay_id[x, c], piece(x, shard(2), b_pos, c))
            b_send(x, 2, c)

    def b_recv(x, dz):
        for c in order(x, -dz % 4):
            for db in (1, 3):
                ref = piece(x, shard(dz), at(b_pos, -db), c)
                arrive(b_id[x, dz, db, c], ref)
                if passed_on(x, db, c):
                    pass_id[x, dz, c] = send(ref, device(db=db))
        for db in (0, 1, 3):
            to_twin(x, piece(x, shard(dz), at(b_pos, db)), piece(x, shard(dz, 1 - core), at(a_pos, db)))

    def b_pass_recv(x, dz):
        for c in order(x, -dz % 4):
            arrive(pass_id[x, dz, c], piece(x, shard(dz), at(b_pos, 2), c))
        to_twin(x, piece(x, shard(dz), at(b_pos, 2)), piece(x, shard(dz, 1 - core), at(a_pos, 2)))

    def deep_send():
        for step in (0, 1):
            for dz, half in ((1, step), (3, 1 - step)):
                deep_id[dz, half] = send(deep(lag, half), device(dz=dz))

    def deep_relay():
        for dz, half in ((1, 0), (3, 1)):
            arrive(deep_id[dz, half], deep(shard(-dz), half))
            deep_id[2, half] = send(deep(shard(-dz), half), device(dz=dz))

    def deep_rest():
        for dz, half in ((1, 1), (3, 0)):
            arrive(deep_id[dz, half], deep(shard(-dz), half))
            to_twin(1, deep(shard(-dz)), deep(shard(-dz, 1 - core)))

    def deep_last():
        for half in (0, 1):
            arrive(deep_id[2, half], deep(shard(2), half))
        to_twin(1, deep(shard(2)), deep(shard(2, 1 - core)))

    def table_done(x):
        for n, ref in twin_in[x]:
            arrive(n, ref)

    def product(x, klass, offset, patch):
        blocks = tables[x][klass, pl.ds(offset, STEPS)]
        window = jnp.concatenate([blocks[m] for m in range(STEPS)], axis=1)
        return jnp.dot(window, hist[patch], preferred_element_type=jnp.float32)

    def pair_copy(x, q):
        da = lax.rem(lax.rem(q, 4) + 1, 4)
        blocks = pl.ds(q * SLOTS, SLOTS)
        return pltpu.make_async_remote_copy(
            src_ref=send_buf.at[x, blocks], dst_ref=recv_buf.at[x, blocks],
            send_sem=pair_send.at[x, q], recv_sem=pair_recv.at[x, q],
            device_id=device(da=da), device_id_type=MESH,
        )

    def served(x):
        @pl.loop(0, SIDE * SIDE // 2)
        def _(step):
            for q in (step * 2, step * 2 + 1):
                da = lax.rem(lax.rem(q, 4) + 1, 4)
                peer = lax.rem(a_pos + da, SIDE) * a_unit + lax.rem(b_pos + q // 4 + 1, SIDE) * b_unit
                for s in range(SLOTS):
                    block = product(x, send_class[s, peer], send_lag[s, peer], send_patch[s, peer])
                    send_buf[x, q * SLOTS + s] = block.astype(jnp.bfloat16)
            pair_copy(x, step * 2).start()

            @pl.when(lax.rem(step, 2) == 0)
            def _():
                pair_copy(x, step * 2 + 1).start()

    def local(x, first, count):
        @pl.loop(first, first + count)
        def _(group):
            @pl.loop(0, GROUP // 4)
            def _(i):
                for s in range(4):
                    j = group * GROUP + i * 4 + s
                    contrib[i * 4 + s] = product(x, local_class[j], local_lag[j], local_src[j])

            @pl.loop(0, HALF // 32)
            def _(chunk):
                rows = pl.ds(pl.multiple_of(chunk * 32, 32), 32)
                totals = [near[x, t, rows, :] for t in range(OWNED)]
                for i in range(GROUP):
                    part = contrib[i, rows, :]
                    target = local_target[group * GROUP + i]
                    for t in range(OWNED):
                        totals[t] += jnp.where(target == t, part, 0.0)
                for t in range(OWNED):
                    near[x, t, rows, :] = totals[t]

    def merge(x, db):
        for r in range(3):
            pair_copy(x, db * 4 + r).wait_recv()

        @pl.loop(0, HALF // 16)
        def _(chunk):
            rows = pl.ds(pl.multiple_of(chunk * 16, 16), 16)
            totals = [None] * OWNED
            for r in range(4):
                da = (r + 1) % 4
                source = at(a_pos, -da)
                buffer = send_buf if da == 0 else recv_buf
                for s in range(SLOTS):
                    part = buffer[x, (db * 4 + r) * SLOTS + s, rows, :].astype(jnp.float32)
                    which = target_row[db, pl.ds(source * SLOTS + s, 1), :]
                    for t in range(OWNED):
                        kept = jnp.where(jnp.broadcast_to(which, part.shape) == t, part, 0.0)
                        totals[t] = kept if totals[t] is None else totals[t] + kept
            for t in range(OWNED):
                if db < 3:
                    merged[x, db * OWNED + t, rows, :] = totals[t].astype(jnp.bfloat16)
                else:
                    near[x, t, rows, :] += totals[t]

        if db < 3:
            merged_copy(x, db).start()

    def merged_copy(x, db):
        blocks = pl.ds(db * OWNED, OWNED)
        return pltpu.make_async_remote_copy(
            src_ref=merged.at[x, blocks], dst_ref=arrived.at[x, blocks],
            send_sem=pair_send.at[x, 16 + db], recv_sem=pair_recv.at[x, 16 + db],
            device_id=device(db=db + 1), device_id_type=MESH,
        )

    def z_one(x, dz, c):
        z_id[x, dz, c] = send(piece(x, lag, b_pos, c), device(dz=dz))

    pl.semaphore_wait(barrier, len(partners))
    for dz, c in ((1, 0), (3, 3), (1, 1), (3, 2)):
        shard_loads[c].wait()
        turn(0, c)
        z_one(0, dz, c)
    for dz, c in ((1, 2), (3, 1), (1, 3), (3, 0)):
        z_one(0, dz, c)
    for c in range(4):
        turn(1, c)
    for x in (0, 1):
        to_twin(x, whole(x, lag), whole(x, shard(0, 1 - core)))
    for dd in (1, 2, 3):
        n = len(copies)
        copies.append(target_own.at[at(b_pos, dd)])
        remote(n, target_own.at[at(b_pos, dd)], target_row.at[3 - dd], device(db=dd)).start()
        target_id[3 - dd] = n
    hist_load.start()
    inverse_load.start()
    incident_load.start()
    zero = jnp.zeros((HALF, PANEL), jnp.float32)
    for x in (0, 1):
        for t in range(OWNED):
            near[x, t] = zero

    z_recv(0)
    z_send(1)
    deep_send()
    b_recv(0, 3)
    b_recv(0, 1)
    z_relay_recv(0)
    b_recv(0, 2)
    z_recv(1)
    for dz in (3, 1, 2):
        b_pass_recv(0, dz)
    hist_load.wait()
    for db in range(3):
        arrive(target_id[db], target_row.at[db])
    table_done(0)

    served(0)
    z_relay_recv(1)
    deep_relay()
    b_recv(1, 3)
    b_recv(1, 1)
    local(0, 0, 2)
    b_recv(1, 2)
    merge(0, 0)
    local(0, 2, 1)
    merge(0, 1)
    for dz in (3, 1, 2):
        b_pass_recv(1, dz)
    deep_rest()
    local(0, 3, 1)
    merge(0, 2)
    deep_last()
    local(0, 4, 1)
    table_done(1)

    served(1)
    merge(0, 3)
    local(0, 5, 1)
    for db in range(3):
        merge(1, db)
        local(1, 2 * db, 2)
    merge(1, 3)
    inverse_load.wait()
    incident_load.wait()
    for x in (0, 1):
        for db in range(3):
            merged_copy(x, db).wait_recv()
    @pl.loop(0, HALF // 16)
    def _(chunk):
        rows = pl.ds(pl.multiple_of(chunk * 16, 16), 16)
        for x in (0, 1):
            whole_rows = pl.ds(pl.multiple_of(x * HALF + chunk * 16, 16), 16)
            for t in range(OWNED):
                total = near[x, t, rows, :]
                for db in range(3):
                    total += arrived[x, db * OWNED + t, rows, :].astype(jnp.float32)
                residual = incident[t, whole_rows, :].astype(jnp.float32) - total
                incident[t, whole_rows, :] = residual.astype(jnp.bfloat16)

    for t in range(OWNED):
        density = jnp.dot(inverse[t], incident[t], preferred_element_type=jnp.float32)
        out_ref[t] = density.astype(jnp.bfloat16)

    for x in (0, 1):
        for db in range(4):
            for r in range(3):
                pair_copy(x, db * 4 + r).wait_send()
        for db in range(3):
            merged_copy(x, db).wait_send()
    for n, ref in enumerate(copies):
        remote(n, ref, ref, twin).wait_send()


def near_field(weights, history, inverse_blocks, incident, tables):
    vmem = pltpu.VMEM
    dma = pltpu.SemaphoreType.DMA
    smem = pl.BlockSpec(memory_space=pltpu.SMEM)
    anywhere = pl.BlockSpec(memory_space=pl.ANY)
    half = jnp.bfloat16
    return pl.pallas_call(
        near_kernel,
        out_shape=jax.ShapeDtypeStruct((OWNED, PANEL, PANEL), half),
        in_specs=[anywhere] * 4 + [smem] * 8,
        out_specs=pl.BlockSpec(memory_space=vmem),
        scratch_shapes=[
            vmem((CLASSES, LAGS, HALF, PANEL), half),
            vmem((CLASSES, LAGS, HALF, PANEL), half),
            vmem((OWNED, STEPS * PANEL, PANEL), half),
            vmem((CLASSES, SHARD, PANEL), half),
            vmem((OWNED, PANEL, PANEL), half),
            vmem((OWNED, PANEL, PANEL), half),
            vmem((2, OWNED, HALF, PANEL), jnp.float32),
            vmem((2, 32, HALF, PANEL), half),
            vmem((2, 32, HALF, PANEL), half),
            vmem((2, 12, HALF, PANEL), half),
            vmem((2, 12, HALF, PANEL), half),
            vmem((GROUP, HALF, PANEL), jnp.float32),
            vmem((SIDE, SIDE * SLOTS, PANEL), jnp.int32),
            vmem((SIDE, SIDE * SLOTS, PANEL), jnp.int32),
            dma((NCOPY,)),
            dma((NCOPY,)),
            dma((2, 19)),
            dma((2, 19)),
            dma((8,)),
        ],
        compiler_params=pltpu.CompilerParams(
            collective_id=0, has_side_effects=True, vmem_limit_bytes=60 * 2**20
        ),
    )(weights, history, inverse_blocks, incident, *tables)


def per_device(
    weights, history, send_patch, send_lag, send_class, recv_target,
    local_src, local_lag, local_class, local_target, inverse_blocks, incident,
):
    return near_field(
        weights, history, inverse_blocks, incident,
        (send_patch.T, send_lag.T, send_class.T, recv_target.T, local_src, local_lag, local_class, local_target),
    )


def solution(mesh):
    both = ("grp", "lag")
    return jax.shard_map(
        per_device,
        mesh=mesh,
        in_specs=(
            P(None, "lag", None), P(both, None, None),
            P(both, None), P(both, None), P(both, None), P(both, None),
            P(both), P(both), P(both), P(both),
            P(both, None, None), P(both, None, None),
        ),
        out_specs=P(both, None, None),
        check_vma=False,
    )
```

time: 104 us -> 91.7 us (0.88)
  Pallas kernels: 100 us -> 89.3 us
  matrix products: 1.56 us -> 0 us
    pallas_call x1, Pallas kernels: 100 us -> 89.3 us  [near_field(): pl.pallas_call(near_kernel, out_shape=jax.ShapeDtypeStruct((OWNED, PANEL,...]
    dot_general x1 -> x0, matrix products: 1.56 us -> none  [per_device(): jnp.einsum('tpq,tqc->tpc', inverse_blocks, residual, preferred_element_ty...]
where the time goes in v3:
time: 91.7 us; the launch traced here: 91.2 us
  Pallas kernels  89.3 us (97%)
  local copies, waits for them, and re-layouts  1.87 us (2%)
    pallas_call x1, Pallas kernels, near_field(): pl.pallas_call(near_kernel, out_shape=jax.ShapeDtypeStruct((OWNED, PANEL,...  89.3 us
    unnamed x1, local copies, waits for them, and re-layouts  1.87 us

profile of v3, /device:TPU:1, one launch (start us, length us, event | category | flops | bytes accessed | tf_op | source)
XLA Modules:
  0.0 91.2 jit_solution(7401402857748926603)
XLA Ops:
  0.0 89.3 %shard_map.118 = bf16[4,256,256]{2,1,0:T(8,128)(2,1)} custom-call(bf16[3,2048,256]{2,1,0:T(8,128)(2,1)} %w_hbm.1, bf16[4,2048,256]{2,1,0:T(8,128)(2,1)} %h_hbm.1, bf16[4,256,256]{2,1,0:T(8,128)(2,1)} %inverse_hbm.1, bf16[4,256,256]{2,1,0:T(8,128)(2,1)} %incident_hbm.1, s32[2,16]{1,0:T(2,128)} %bitcast.4, s32[2,16]{1,0:T(2,128)} %bitcast.5, s32[2,16]{1,0:T(2,128)} %bitcast.6, ...), custom_call_target="tpu_custom_call" | custom-call | tf_op jit(solution)/shard_map/pallas_call | solution.py:390
  89.3 1.9 %copy.14 = bf16[4,256,256]{2,1,0:T(8,128)(2,1)} copy(bf16[4,256,256]{2,1,0:T(8,128)(2,1)} %shard_map.118) | data formatting | bytes 1048576

commit v4 on v3

--- a/solution.py
+++ b/solution.py
@@ -104,13 +104,6 @@
     for p in partners:
         pl.semaphore_signal(barrier, inc=1, device_id=p, device_id_type=MESH)
 
-    for b in range(SIDE):
-        for a in range(SIDE):
-            for s in range(SLOTS):
-                value = recv_target[s, a * a_unit + b * b_unit]
-                target_own[b, pl.ds(a * SLOTS + s, 1), :] = jnp.full((1, PANEL), value, jnp.int32)
-    target_row[3] = target_own[b_pos]
-
     def turn(x, c):
         @pl.loop(0, 2 * CLASSES)
         def _(n):
@@ -292,6 +285,13 @@
         z_one(0, dz, c)
     for dz, c in ((1, 2), (3, 1), (1, 3), (3, 0)):
         z_one(0, dz, c)
+    for b in range(SIDE):
+        for a in range(SIDE):
+            for s in range(SLOTS):
+                value = recv_target[s, a * a_unit + b * b_unit]
+                target_own[b, pl.ds(a * SLOTS + s, 1), :] = jnp.full((1, PANEL), value, jnp.int32)
+    target_row[3] = target_own[b_pos]
+
     for c in range(4):
         turn(1, c)
     for x in (0, 1):

time: 91.7 us -> 91.7 us (level)
  no operation moved by 1% of the time
where the time goes in v4:
time: 91.7 us; the launch traced here: 91.2 us
  Pallas kernels  89.3 us (97%)
  local copies, waits for them, and re-layouts  1.87 us (2%)
    pallas_call x1, Pallas kernels, near_field(): pl.pallas_call(near_kernel, out_shape=jax.ShapeDtypeStruct((OWNED, PANEL,...  89.3 us
    unnamed x1, local copies, waits for them, and re-layouts  1.87 us

profile of v4, /device:TPU:1, one launch (start us, length us, event | category | flops | bytes accessed | tf_op | source)
XLA Modules:
  0.0 91.2 jit_solution(14317364035384902038)
XLA Ops:
  0.0 89.3 %shard_map.118 = bf16[4,256,256]{2,1,0:T(8,128)(2,1)} custom-call(bf16[3,2048,256]{2,1,0:T(8,128)(2,1)} %w_hbm.1, bf16[4,2048,256]{2,1,0:T(8,128)(2,1)} %h_hbm.1, bf16[4,256,256]{2,1,0:T(8,128)(2,1)} %inverse_hbm.1, bf16[4,256,256]{2,1,0:T(8,128)(2,1)} %incident_hbm.1, s32[2,16]{1,0:T(2,128)} %bitcast.4, s32[2,16]{1,0:T(2,128)} %bitcast.5, s32[2,16]{1,0:T(2,128)} %bitcast.6, ...), custom_call_target="tpu_custom_call" | custom-call | tf_op jit(solution)/shard_map/pallas_call | solution.py:390
  89.3 1.9 %copy.14 = bf16[4,256,256]{2,1,0:T(8,128)(2,1)} copy(bf16[4,256,256]{2,1,0:T(8,128)(2,1)} %shard_map.118) | data formatting | bytes 1048576
